TPU v7x, 768 devices: a whole 4x8x12 slice. The times are simulated.
768 devices in a mesh: wide: 48 (over z, y_hi, core), blk: 16 (over x, y_lo).
Axes of the slice: x: 4, y: 8 (y_hi: 2, y_lo: 4; y = y_hi * 4 + y_lo), z: 12, core: 2. Of those that a mesh axis runs over, the one named last changes fastest.
Arguments:
- query_emb: bfloat16 [3072, 4096], P(('wide', 'blk')), may hold values from -0.1875 to 0.1875
- passage_emb: bfloat16 [3072, 4096], P(('wide', 'blk')), may hold values from -0.1875 to 0.1875
- row_lse: float32 [3072], P('wide'), may hold values from 2.5 to 4.5
- positive: int32 [3072], P('wide'), may hold values from 0 to 63
- token_lengths: int32 [48, 64], P('wide'), may hold values from 1 to 16, 192 in all within a row
- destination: int32 [9216, 1], P('wide'), may hold values from 0 to 47; in each aligned block of 192 rows (0 to 191, 192 to 383, ...) at most 6 rows name the same one
- mlp_act: bfloat16 [9216, 12288], P('wide', 'blk'), may hold values from -6 to 6
- resid: bfloat16 [9216, 4096], P('wide', 'blk'), may hold values from -6 to 6
- w_down: bfloat16 [12288, 4096], P('blk'), may hold values from -0.054126588 to 0.054126588
- gain: float32 [4096], P('blk'), may hold values from 0.1 to 1.9
Outputs:
- query_grad: bfloat16 [3072, 4096], P(('wide', 'blk'))
- resid_grad: bfloat16 [13824, 4096], P('wide', 'blk')
- act_grad: bfloat16 [13824, 12288], P('wide', 'blk')
- normed_out: bfloat16 [13824, 4096], P('wide', 'blk')
Inputs may be any that keep to these rules, and one draw needn't show every extreme that they name: `token_lengths`: each row lists the token counts of the group's 64 passages in order and sums to 192. Among the token rows of one group, at most 6 name the same destination.
All inputs are finite; a program needn't handle non-finite values.
Results may differ from a plain program's by a relative error of at most 0.02.
Values may be sent and summed in bfloat16 or wider, within the bound.
A program may use at most 32 MiB of HBM per device.

v0:
```python
import jax
import jax.numpy as jnp
from jax import lax
from jax.sharding import PartitionSpec as P

logit_scale = 24.0
norm_eps = 1e-06


def coefficients(scores, lse_part, pos_part):
    columns = lax.broadcasted_iota(jnp.int32, scores.shape, 1)
    target = (pos_part[:, None] == columns).astype(jnp.float32)
    return (jnp.exp(scores - lse_part[:, None]) - target).astype(jnp.bfloat16)


def norm_layer(act_rows, resid_rows, grad_rows, w_down, gain):
    feat_width = resid_rows.shape[1]
    features = w_down.shape[1]
    offset = lax.axis_index("blk") * feat_width
    partial_terms = jnp.dot(act_rows, w_down, preferred_element_type=jnp.float32)
    own_columns = lax.dynamic_slice_in_dim(
        partial_terms, offset, feat_width, 1
    ) + resid_rows.astype(jnp.float32)
    partial_terms = lax.dynamic_update_slice_in_dim(partial_terms, own_columns, offset, 1)
    hidden = lax.psum_scatter(
        partial_terms.astype(jnp.bfloat16), "blk", scatter_dimension=1, tiled=True
    ).astype(jnp.float32)
    gained = gain[None, :] * grad_rows.astype(jnp.float32)
    squares, inner_sum = lax.psum(
        (jnp.sum(hidden * hidden, axis=1), jnp.sum(gained * hidden, axis=1)), "blk"
    )
    inv_rms = lax.rsqrt(squares / features + norm_eps)[:, None]
    inner_sum = inner_sum[:, None]
    normed = (gain[None, :] * hidden * inv_rms).astype(jnp.bfloat16)
    resid_back = (
        inv_rms * gained - hidden * (inv_rms * inv_rms * inv_rms) * inner_sum / features
    ).astype(jnp.bfloat16)
    act_back = lax.dot_general(
        lax.all_gather(resid_back, "blk", axis=1, tiled=True),
        w_down,
        (((1,), (1,)), ((), ())),
        preferred_element_type=jnp.float32,
    )
    return (resid_back, act_back.astype(jnp.bfloat16), normed)


def shards(
    query_emb,
    passage_emb,
    row_lse,
    positive,
    token_lengths,
    destination,
    mlp_act,
    resid,
    w_down,
    gain,
):
    pair_rows = query_emb.shape[0]
    feat_width = resid.shape[1]
    hid_width = w_down.shape[0]
    blk_index = lax.axis_index("blk")
    first_row = blk_index * pair_rows
    query_all, passage_all = (
        lax.all_gather(query_emb, "blk", axis=0, tiled=True),
        lax.all_gather(passage_emb, "blk", axis=0, tiled=True),
    )
    scores = logit_scale * jnp.dot(query_all, passage_all.T, preferred_element_type=jnp.float32)
    coef_full = coefficients(scores, row_lse, positive)
    own_coef = lax.dynamic_slice_in_dim(coef_full, first_row, pair_rows, 0)
    query_grad = (
        logit_scale * jnp.dot(own_coef, passage_all, preferred_element_type=jnp.float32)
    ).astype(jnp.bfloat16)
    query_cols = lax.dynamic_slice_in_dim(query_all, blk_index * feat_width, feat_width, 1)
    grad_cols = logit_scale * lax.dot_general(
        query_cols, coef_full, (((0,), (0,)), ((), ())), preferred_element_type=jnp.float32
    )
    lengths_row = token_lengths[0]
    starts = jnp.cumsum(lengths_row) - lengths_row
    tok_count = resid.shape[0]
    positions = lax.broadcasted_iota(jnp.int32, (tok_count, lengths_row.shape[0]), 0)
    member = (positions >= starts[None, :]) & (positions < (starts + lengths_row)[None, :])
    weights = member.astype(jnp.float32) * (1.0 / lengths_row.astype(jnp.float32))[None, :]
    tok_grad = lax.dot_general(
        weights,
        grad_cols,
        (((1,), (1,)), ((), ())),
        precision=lax.Precision.HIGHEST,
        preferred_element_type=jnp.float32,
    ).astype(jnp.bfloat16)
    wide_count = lax.axis_size("wide")
    slot_count = 3 * tok_count // (2 * wide_count)
    dest_hot = (destination == lax.broadcasted_iota(jnp.int32, (tok_count, wide_count), 1)).astype(
        jnp.int32
    )
    rank_of = jnp.cumsum(dest_hot, axis=0) - dest_hot
    slot_of = jnp.sum(rank_of * dest_hot, axis=1) + destination[:, 0] * slot_count
    placer = (
        lax.broadcasted_iota(jnp.int32, (wide_count * slot_count, tok_count), 0) == slot_of[None, :]
    ).astype(jnp.bfloat16)
    payload = jnp.concatenate([mlp_act, resid, tok_grad], axis=1)
    packed = jnp.dot(placer, payload, preferred_element_type=jnp.float32).astype(jnp.bfloat16)
    packed = packed.reshape(wide_count, slot_count, hid_width + 2 * feat_width)
    arrived = lax.all_to_all(packed, "wide", split_axis=0, concat_axis=0, tiled=True).reshape(
        wide_count * slot_count, hid_width + 2 * feat_width
    )
    resid_grad, act_grad, normed_out = norm_layer(
        arrived[:, :hid_width],
        arrived[:, hid_width : hid_width + feat_width],
        arrived[:, hid_width + feat_width :],
        w_down,
        gain,
    )
    return (query_grad, resid_grad, act_grad, normed_out)


def solution(mesh):
    return jax.shard_map(
        shards,
        mesh=mesh,
        in_specs=(
            P(("wide", "blk"), None),
            P(("wide", "blk"), None),
            P("wide"),
            P("wide"),
            P("wide", None),
            P("wide", None),
            P("wide", "blk"),
            P("wide", "blk"),
            P("blk", None),
            P("blk"),
        ),
        out_specs=(P(("wide", "blk"), None), P("wide", "blk"), P("wide", "blk"), P("wide", "blk")),
        check_vma=False,
    )
```

profile of v0, /device:TPU:62, one launch (start us, length us, event | category | flops | bytes accessed | tf_op | source)
XLA Modules:
  0.0 409.2 jit_solution(4726022978902431655)
XLA Ops:
  7.2 0.7 divide_bitcast_fusion
  8.0 0.7 iota_compare_fusion.5
  8.7 0.7 copy.20
  9.4 0.1 reduce-window.14
  9.5 0.1 reduce.1
  9.6 0.7 fusion.34
  10.3 0.6 reduce-window.10
  10.9 0.2 slice_reduce_fusion
  11.1 0.1 bitcast_bitcast_fusion
  11.2 0.7 fusion.25
  11.9 0.7 multiply_add_fusion
  12.6 41.6 %all-gather = bf16[16,4,4096]{2,1,0:T(4,128)(2,1)S(1)} all-gather(bf16[1,4,4096]{2,1,0:T(4,128)(2,1)} %bitcast.32), channel_id=1, replica_groups=mesh['wide'=48,'blk'=16] {'blk'}, dimensions={0}, use_global_device_ids=true | all-gather | bytes 557056 | tf_op jit(solution)/shard_map/all_gather | solution.py:65
  54.2 0.1 reshape.56
  54.4 44.5 %all-gather.1 = bf16[16,4,4096]{2,1,0:T(4,128)(2,1)S(1)} all-gather(bf16[1,4,4096]{2,1,0:T(4,128)(2,1)} %bitcast.33), channel_id=1, replica_groups=mesh['wide'=48,'blk'=16] {'blk'}, dimensions={0}, use_global_device_ids=true | all-gather | bytes 557056 | tf_op jit(solution)/shard_map/all_gather | solution.py:66
  98.8 0.1 reshape.58
  99.0 1.0 fusion.4
  99.9 0.2 convolution_multiply_fusion.1
  100.2 0.3 convolution_convert_fusion.2
  100.5 0.4 convolution_convert_fusion
  100.8 0.2 reshape.52
  101.1 58.4 %all_to_all.5 = bf16[48,6,1280]{2,1,0:T(8,128)(2,1)S(1)} all-to-all(bf16[48,6,1280]{2,1,0:T(8,128)(2,1)S(1)} %reshape.52), channel_id=1, replica_groups=mesh['wide'=48,'blk'=16] {'wide'}, dimensions={0} | all-to-all | bytes 1474560 | tf_op jit(solution)/shard_map/all_to_all | solution.py:104
  159.5 0.2 reshape.53
  159.7 4.8 %fusion.10 = f32[288,4096]{1,0:T(8,128)S(1)} fusion(bf16[768,4096]{1,0:T(8,128)(2,1)} %param.18, bf16[288,1280]{1,0:T(8,128)(2,1)S(1)} %reshape.53), kind=kOutput, calls=%fused_computation.20 | convolution fusion | flops 1811939328 | bytes 11452416 | tf_op jit(solution)/shard_map/dot_general | solution.py:20
  164.5 0.1 add_dynamic-update-slice_fusion
  164.6 1.7 convert_element_type.54
  166.4 91.9 %reduce-scatter.2.cloned.1.call-done = bf16[288,256]{1,0:T(8,128)(2,1)} async-done(((bf16[288,4096]{1,0:T(8,128)(2,1)}), bf16[288,256]{1,0:T(8,128)(2,1)}) %reduce-scatter.2.cloned.1.call-update) | async-done | bytes 147472 | tf_op jit(solution)/shard_map/reduce_scatter | solution.py:25
  258.3 1.1 fusion.12
  259.4 37.7 %all-reduce.1 = (f32[288]{0:T(512)S(1)}, f32[288]{0:T(512)S(1)}) all-reduce(f32[288]{0:T(512)S(1)} %get-tuple-element.5, f32[288]{0:T(512)S(1)} %get-tuple-element.4), channel_id=1, replica_groups=mesh['wide'=48,'blk'=16] {'blk'}, use_global_device_ids=true, to_apply=%region_8.9 | all-reduce | flops 576 | bytes 4608 | tf_op jit(solution)/shard_map/psum | solution.py:29
  297.2 1.8 fusion.19
  299.0 0.8 fusion
  299.8 96.3 %all-gather.4.cloned.1.call-done = bf16[288,4096]{1,0:T(8,128)(2,1)} async-done(((bf16[288,256]{1,0:T(8,128)(2,1)}), bf16[288,4096]{1,0:T(8,128)(2,1)}) %all-gather.4.cloned.1.call-update) | async-done | bytes 2359312 | tf_op jit(solution)/shard_map/all_gather | solution.py:39
  396.1 6.3 %convolution_convert_fusion.1 = bf16[288,768]{1,0:T(8,128)(2,1)} fusion(bf16[288,4096]{1,0:T(8,128)(2,1)} %all-gather.4.cloned.1.call-done, bf16[768,4096]{1,0:T(8,128)(2,1)} %param.18), kind=kOutput, calls=%fused_computation.3 | convolution fusion | flops 1812160512 | bytes 9093120 | tf_op jit(solution)/shard_map/dot_general | solution.py:38
  (14 shorter events, 0.2 us)
Async XLA Ops:
  7.2 93.3 %copy-start.2 = (bf16[192,256]{1,0:T(8,128)(2,1)S(1)}, bf16[192,256]{1,0:T(8,128)(2,1)}, u32[]{:S(2)}) copy-start(bf16[192,256]{1,0:T(8,128)(2,1)} %param.17) | copy-start | bytes 294916
  7.2 93.3 %copy-start.1 = (bf16[192,768]{1,0:T(8,128)(2,1)S(1)}, bf16[192,768]{1,0:T(8,128)(2,1)}, u32[]{:S(2)}) copy-start(bf16[192,768]{1,0:T(8,128)(2,1)} %param.16) | copy-start | bytes 884740
  7.2 251.1 %reduce-scatter.2.cloned.1.call-start = ((), (), s32[]{:S(2)}) async-start(), calls=%async_computation.2 | async-start | bytes 2506752 | tf_op jit(solution)/shard_map/reduce_scatter | solution.py:25
  164.6 93.7 %copy-start = (f32[256]{0:T(256)S(1)}, f32[256]{0:T(256)}, u32[]{:S(2)}) copy-start(f32[256]{0:T(256)} %param.19) | copy-start | bytes 3076
  166.4 229.7 %all-gather.4.cloned.1.call-start = ((), (), s32[]{:S(2)}) async-start(), calls=%async_computation.3 | async-start | bytes 2506752 | tf_op jit(solution)/shard_map/all_gather | solution.py:39
Sparse Core Ops, SparseCore 0:
  166.5 91.7 reduce-scatter.1
  299.1 96.9 all-gather.3
where the time goes:
time: 410 us; the launch traced here: 409 us
  waiting for transfers between devices  188 us (46%)
  blocking collectives  182 us (44%)
  between operations  14.2 us (3%)
  matrix products  13.7 us (3%)
  other arithmetic  9.14 us (2%)
    all_gather x1, waiting for transfers between devices, norm_layer(): lax.all_gather(resid_back, 'blk', axis=1, tiled=True)  96.3 us
    reduce_scatter x1, waiting for transfers between devices, norm_layer(): lax.psum_scatter(partial_terms.astype(jnp.bfloat16), 'blk', scatter_dimen...  91.9 us
    all_to_all x1, blocking collectives, shards(): lax.all_to_all(packed, 'wide', split_axis=0, concat_axis=0, tiled=True)  58.4 us
    all_gather x1, blocking collectives, shards(): lax.all_gather(passage_emb, 'blk', axis=0, tiled=True)  44.5 us
    all_gather x1, blocking collectives, shards(): lax.all_gather(query_emb, 'blk', axis=0, tiled=True)  41.6 us
    psum x1, blocking collectives, norm_layer(): lax.psum((jnp.sum(hidden * hidden, axis=1), jnp.sum(gained * hidden, axis...  37.7 us
  transfers between devices with their start and end apart: 2, of which 2 were waited for; matrix products, arithmetic and copies ran while one was open for 0% of the time, Pallas kernels for 0%

commit v1 on v0

v1 whole, which is shorter than its diff:
```python
import functools

import jax
import jax.numpy as jnp
from jax import lax
from jax.experimental import pallas as pl
from jax.experimental.pallas import tpu as pltpu
from jax.sharding import PartitionSpec as P

logit_scale = 24.0
norm_eps = 1e-06
MESH = pl.DeviceIdType.MESH
N = 16
F32 = jnp.float32
BF16 = jnp.bfloat16
HIGH = lax.Precision.HIGHEST
ORDER = (2, 3, 1, 0)


def nt(a, b, precision=None):
    return lax.dot_general(
        a, b, (((1,), (1,)), ((), ())), precision=precision, preferred_element_type=F32
    )


def tn(a, b, precision=None):
    return lax.dot_general(
        a, b, (((0,), (0,)), ((), ())), precision=precision, preferred_element_type=F32
    )


def iota(shape, dim):
    return lax.broadcasted_iota(jnp.int32, shape, dim)


def partner(i, m):
    if m == 0:
        return i
    if m == 1:
        return i + 1 - 2 * lax.rem(i, 2)
    if m == 2:
        return lax.rem(i + 2, 4)
    return 3 - i


def kernel(
    q_ref, p_ref, lse_ref, pos_ref, len_ref, gain_ref, act_hbm, resid_hbm, w_hbm,
    qg_ref, out_ref,
    act, resid, w, emb, emb_all, part, ra, sb, rb, sy, ry, sc, sc_all, qgs, qgr, st, st_all, ag, acc,
    ld_sem, w_sem, emb_s, emb_r, sc_s, sc_r, st_s, st_r, qg_s, qg_r,
    a_s, a_r, b_s, b_r, y_s, y_r, gy_s, gx_s, gf_s, g_r,
):
    me = lax.axis_index("blk")
    x, y = lax.div(me, 4), lax.rem(me, 4)
    xs = [partner(x, m) for m in range(4)]
    ys = [partner(y, m) for m in range(4)]
    tok, width = resid.shape
    half = tok // 2
    pairs = lse_ref.shape[1]

    def remote(src, dst, send, recv, peer):
        return pltpu.make_async_remote_copy(
            src_ref=src, dst_ref=dst, send_sem=send, recv_sem=recv,
            device_id={"blk": peer}, device_id_type=MESH,
        )

    def cols(i):
        return pl.ds(pl.multiple_of(i * width, width), width)

    def rows8(i):
        return pl.ds(pl.multiple_of(i * 8, 8), 8)

    def each_peer(body):
        def step(o, carry):
            body(lax.rem(me + o, N))
            return carry

        lax.fori_loop(1, N, step, 0)

    ld_act = pltpu.make_async_copy(act_hbm, act, ld_sem.at[0])
    ld_act.start()
    ld_resid = pltpu.make_async_copy(resid_hbm, resid, ld_sem.at[1])
    ld_resid.start()

    def ld_w(b):
        return pltpu.make_async_copy(w_hbm.at[:, cols(b)], w.at[b], w_sem.at[b])

    for m in ORDER:
        for d in range(4):
            ld_w(d * 4 + ys[m]).start()

    barrier = pltpu.get_barrier_semaphore()
    each_peer(
        lambda peer: pl.semaphore_signal(
            barrier, inc=1, device_id={"blk": peer}, device_id_type=MESH
        )
    )
    emb[0:4, :] = q_ref[...].astype(F32)
    emb[4:8, :] = p_ref[...].astype(F32)
    emb_all[rows8(me), :] = emb[:, cols(me)]

    def term(b):
        ld_w(b).wait()
        part[b] = jnp.dot(act[...], w[b], preferred_element_type=F32).astype(BF16)

    ld_act.wait()
    for d in range(4):
        term(d * 4 + ys[ORDER[0]])
    pl.semaphore_wait(barrier, N - 1)

    def emb_copy(peer):
        return remote(
            emb.at[:, cols(peer)], emb_all.at[rows8(me), :], emb_s.at[peer], emb_r.at[me], peer
        )

    def emb_got(peer):
        return remote(
            emb.at[:, cols(peer)], emb_all.at[rows8(peer), :], emb_s.at[peer], emb_r.at[peer], peer
        )

    each_peer(lambda peer: emb_copy(peer).start())

    rows = (pl.ds(0, half), pl.ds(half, half))
    first = (1, 3)

    def a_copy(k, h, s):
        m = ORDER[k]
        block = xs[first[h]] if s == 0 else xs[2]
        return remote(
            part.at[block * 4 + ys[m], rows[h]], ra.at[k, h, s],
            a_s.at[k * 4 + h * 2 + s], a_r.at[k * 4 + h * 2 + s],
            xs[first[h]] * 4 + y,
        )

    def b_copy(k, h):
        return remote(
            sb.at[k, h], rb.at[k, h], b_s.at[k * 2 + h], b_r.at[k * 2 + h],
            xs[4 - first[h]] * 4 + y,
        )

    def y_copy(k):
        m = ORDER[k]
        return remote(sy.at[k], ry.at[k], y_s.at[k], y_r.at[k], x * 4 + ys[m])

    for k in range(4):
        if k > 0:
            for d in range(4):
                term(d * 4 + ys[ORDER[k]])
        for s in (1, 0):
            for h in range(2):
                a_copy(k, h, s).start()

    each_peer(lambda peer: emb_got(peer).wait_recv())
    e16 = emb_all[...].astype(BF16)
    r_of = iota((pairs, 8 * N), 0)
    c_of = iota((pairs, 8 * N), 1)
    q_at = lax.div(r_of, 4) * 8 + lax.rem(r_of, 4)
    pick_q = (c_of == q_at).astype(F32).astype(BF16)
    pick_p = (c_of == q_at + 4).astype(F32).astype(BF16)
    q_cols = jnp.dot(pick_q, e16, preferred_element_type=F32).astype(BF16)
    p_cols = jnp.dot(pick_p, e16, preferred_element_type=F32).astype(BF16)
    sc[...] = nt(q_cols, p_cols)
    sc_all[me] = sc[...]

    def sc_copy(peer):
        return remote(sc, sc_all.at[me], sc_s.at[peer], sc_r.at[me], peer)

    def sc_got(peer):
        return remote(sc, sc_all.at[peer], sc_s.at[peer], sc_r.at[peer], peer)

    each_peer(lambda peer: sc_copy(peer).start())

    for k in range(4):
        m = ORDER[k]
        for h in range(2):
            a_copy(k, h, 1).wait_recv()
            block = xs[4 - first[h]] * 4 + ys[m]
            sb[k, h] = (
                part[block, rows[h], :].astype(F32) + ra[k, h, 1].astype(F32)
            ).astype(BF16)
            b_copy(k, h).start()

    each_peer(lambda peer: sc_got(peer).wait_recv())
    total = sc_all[0]
    for i in range(1, N):
        total = total + sc_all[i]
    scores = logit_scale * total
    eye = iota((pairs, pairs), 0) == iota((pairs, pairs), 1)
    lse = jnp.sum(jnp.where(eye, lse_ref[...], 0.0), axis=1, keepdims=True)
    pos = jnp.sum(jnp.where(eye, pos_ref[...].astype(F32), 0.0), axis=1, keepdims=True)
    target = jnp.where(pos == iota((pairs, pairs), 1).astype(F32), 1.0, 0.0)
    coef = (jnp.exp(scores - lse) - target).astype(BF16)
    rr, cc = iota((8 * N, pairs), 0), iota((8 * N, pairs), 1)
    spread = jnp.where(
        (lax.rem(rr, 8) < 4) & (cc == lax.div(rr, 8) * 4 + lax.rem(rr, 8)), 1.0, 0.0
    ).astype(BF16)
    coef_rows = jnp.dot(spread, coef, preferred_element_type=F32).astype(BF16)
    qgs[...] = logit_scale * jnp.dot(coef_rows, p_cols, preferred_element_type=F32)
    qgr[:, cols(me)] = qgs[rows8(me), :]

    def qg_copy(peer):
        return remote(
            qgs.at[rows8(peer), :], qgr.at[:, cols(me)], qg_s.at[peer], qg_r.at[me], peer
        )

    def qg_got(peer):
        return remote(
            qgs.at[rows8(peer), :], qgr.at[:, cols(peer)], qg_s.at[peer], qg_r.at[peer], peer
        )

    pass_grad = logit_scale * tn(coef, q_cols)
    lens = len_ref[...].astype(F32)
    below = jnp.where(iota((pairs, pairs), 0) < iota((pairs, pairs), 1), 1.0, 0.0)
    starts = jnp.dot(
        jnp.broadcast_to(lens, (8, pairs)), below, precision=HIGH, preferred_element_type=F32
    )[0:1, :]
    at = iota((tok, pairs), 0).astype(F32)
    weights = jnp.where((at >= starts) & (at < starts + lens), 1.0 / lens, 0.0)
    tok_grad = jnp.dot(weights, pass_grad, precision=HIGH, preferred_element_type=F32)
    gained = gain_ref[...] * tok_grad.astype(BF16).astype(F32)

    own = None
    for k in range(4):
        m = ORDER[k]
        block = x * 4 + ys[m]
        sums = []
        for h in range(2):
            a_copy(k, h, 0).wait_recv()
            b_copy(k, h).wait_recv()
            sums.append(
                part[block, rows[h], :].astype(F32)
                + ra[k, h, 0].astype(F32)
                + rb[k, h].astype(F32)
            )
        if m != 0:
            for h in range(2):
                sy[k, rows[h], :] = sums[h].astype(BF16)
            y_copy(k).start()
        else:
            own = jnp.concatenate(sums, axis=0)
    each_peer(lambda peer: qg_copy(peer).start())
    ld_resid.wait()
    hidden = own + resid[...].astype(F32)
    for k in range(3):
        y_copy(k).wait_recv()
        hidden = hidden + ry[k].astype(F32)

    ones = jnp.ones((8, width), F32)
    squares = nt(ones, hidden * hidden, HIGH)
    inner = nt(ones, gained * hidden, HIGH)
    st[...] = jnp.where(iota((8, tok), 0) == 0, squares, inner)
    st_all[me] = st[...]

    def st_copy(peer):
        return remote(st, st_all.at[me], st_s.at[peer], st_r.at[me], peer)

    def st_got(peer):
        return remote(st, st_all.at[peer], st_s.at[peer], st_r.at[peer], peer)

    each_peer(lambda peer: st_copy(peer).start())
    each_peer(lambda peer: st_got(peer).wait_recv())
    stat = st_all[0]
    for i in range(1, N):
        stat = stat + st_all[i]
    features = N * width
    row = iota((8, tok), 0)
    inv = lax.rsqrt(stat / features + norm_eps)[0:1, :]
    scale = inv * inv * inv * stat[1:2, :] / features
    both = jnp.where(row == 0, inv, jnp.where(row == 1, scale, 0.0))
    pick = iota((8, width), 0)
    inv_rms = tn(both, jnp.where(pick == 0, 1.0, 0.0), HIGH)
    scale_c = tn(both, jnp.where(pick == 1, 1.0, 0.0), HIGH)
    resid_back = (inv_rms * gained - hidden * scale_c).astype(BF16)
    ag[me] = resid_back

    def gy_copy(m):
        return remote(ag.at[me], ag.at[me], gy_s.at[m], g_r.at[me * 2], x * 4 + ys[m])

    def gy_got(m):
        b = x * 4 + ys[m]
        return remote(ag.at[b], ag.at[b], gy_s.at[m], g_r.at[b * 2], b)

    def gx_copy(m, n):
        b = x * 4 + ys[m]
        return remote(
            ag.at[b], ag.at[b], gx_s.at[m * 2 + n // 2], g_r.at[b * 2], xs[n] * 4 + y
        )

    def gx_got(m, n):
        b = xs[n] * 4 + ys[m]
        return remote(
            ag.at[b], ag.at[b], gx_s.at[m * 2 + n // 2], g_r.at[b * 2], xs[n] * 4 + y
        )

    def gf_copy(m, h):
        b = xs[4 - first[h]] * 4 + ys[m]
        return remote(
            ag.at[b, rows[h]], ag.at[b, rows[h]], gf_s.at[m * 2 + h], g_r.at[b * 2 + h],
            xs[first[h]] * 4 + y,
        )

    def gf_got(m, h):
        b = xs[2] * 4 + ys[m]
        return remote(
            ag.at[b, rows[h]], ag.at[b, rows[h]], gf_s.at[m * 2 + h], g_r.at[b * 2 + h],
            xs[first[h]] * 4 + y,
        )

    for m in (2, 3, 1):
        gy_copy(m).start()
    for n in (1, 3):
        gx_copy(0, n).start()
    normed = (gain_ref[...] * hidden * inv_rms).astype(BF16)
    out_ref[:, 3 * width : 4 * width] = resid_back
    out_ref[:, 4 * width : 5 * width] = normed
    acc[...] = nt(resid_back, w[me])

    def use(b):
        acc[...] += nt(ag[b], w[b])

    def column(m):
        gy_got(m).wait_recv()
        for n in (1, 3):
            gx_copy(m, n).start()
        use(x * 4 + ys[m])

    def neighbours(m):
        for h in range(2):
            n = 4 - first[h]
            gx_got(m, n).wait_recv()
            gf_copy(m, h).start()
        for n in (1, 3):
            use(xs[n] * 4 + ys[m])

    column(1)
    neighbours(0)
    column(2)
    neighbours(1)
    column(3)
    neighbours(2)
    neighbours(3)
    for m in range(4):
        for h in range(2):
            gf_got(m, h).wait_recv()
        use(xs[2] * 4 + ys[m])
    out_ref[:, 0 : 3 * width] = acc[...].astype(BF16)

    each_peer(lambda peer: qg_got(peer).wait_recv())
    qg_ref[...] = qgr[0:4, :].astype(BF16)

    def sent(peer):
        emb_copy(peer).wait_send()
        sc_copy(peer).wait_send()
        st_copy(peer).wait_send()
        qg_copy(peer).wait_send()

    each_peer(sent)
    for k in range(4):
        for h in range(2):
            for s in range(2):
                a_copy(k, h, s).wait_send()
            b_copy(k, h).wait_send()
            gf_copy(k, h).wait_send()
        for n in (1, 3):
            gx_copy(k, n).wait_send()
        if k < 3:
            y_copy(k).wait_send()
            gy_copy(k + 1).wait_send()


def layer(query_emb, passage_emb, lse, pos, lens, gain, act, resid, w_down):
    tok, width = resid.shape
    hid = act.shape[1]
    features = w_down.shape[1]
    pairs = lse.shape[1]
    half = tok // 2
    dma = pltpu.SemaphoreType.DMA
    vmem = pl.BlockSpec(memory_space=pltpu.VMEM)
    hbm = pl.BlockSpec(memory_space=pl.ANY)
    return pl.pallas_call(
        kernel,
        out_shape=(
            jax.ShapeDtypeStruct(query_emb.shape, BF16),
            jax.ShapeDtypeStruct((tok, hid + 2 * width), BF16),
        ),
        in_specs=[vmem] * 6 + [hbm] * 3,
        out_specs=(vmem, vmem),
        scratch_shapes=[
            pltpu.VMEM((tok, hid), BF16),
            pltpu.VMEM((tok, width), BF16),
            pltpu.VMEM((N, hid, width), BF16),
            pltpu.VMEM((8, features), F32),
            pltpu.VMEM((8 * N, width), F32),
            pltpu.VMEM((N, tok, width), BF16),
            pltpu.VMEM((4, 2, 2, half, width), BF16),
            pltpu.VMEM((4, 2, half, width), BF16),
            pltpu.VMEM((4, 2, half, width), BF16),
            pltpu.VMEM((3, tok, width), BF16),
            pltpu.VMEM((3, tok, width), BF16),
            pltpu.VMEM((pairs, pairs), F32),
            pltpu.VMEM((N, pairs, pairs), F32),
            pltpu.VMEM((8 * N, width), F32),
            pltpu.VMEM((8, features), F32),
            pltpu.VMEM((8, tok), F32),
            pltpu.VMEM((N, 8, tok), F32),
            pltpu.VMEM((N, tok, width), BF16),
            pltpu.VMEM((tok, hid), F32),
            dma((2,)), dma((N,)),
            dma((N,)), dma((N,)), dma((N,)), dma((N,)), dma((N,)), dma((N,)), dma((N,)), dma((N,)),
            dma((16,)), dma((16,)), dma((8,)), dma((8,)), dma((4,)), dma((4,)),
            dma((4,)), dma((8,)), dma((8,)), dma((2 * N,)),
        ],
        compiler_params=pltpu.CompilerParams(
            collective_id=0, has_side_effects=True, vmem_limit_bytes=48 * 1024 * 1024
        ),
    )(query_emb, passage_emb, lse, pos, lens, gain, act, resid, w_down)


def shards(
    query_emb,
    passage_emb,
    row_lse,
    positive,
    token_lengths,
    destination,
    mlp_act,
    resid,
    w_down,
    gain,
):
    tok, feat = resid.shape
    hid = mlp_act.shape[1]
    query_grad, payload = layer(
        query_emb, passage_emb, row_lse[None, :], positive[None, :], token_lengths, gain[None, :],
        mlp_act, resid, w_down,
    )
    wide_count = lax.axis_size("wide")
    slot_count = 3 * tok // (2 * wide_count)
    dest_hot = (destination == lax.broadcasted_iota(jnp.int32, (tok, wide_count), 1)).astype(F32)
    lower = (iota((tok, tok), 1) < iota((tok, tok), 0)).astype(F32)
    rank_of = jnp.dot(lower, dest_hot, preferred_element_type=F32)
    rank = jnp.sum(rank_of * dest_hot, axis=1).astype(jnp.int32)
    slot_of = rank + destination[:, 0] * slot_count
    placer = (iota((wide_count * slot_count, tok), 0) == slot_of[None, :]).astype(BF16)
    packed = jnp.dot(placer, payload, preferred_element_type=F32).astype(BF16)
    packed = packed.reshape(wide_count, slot_count, hid + 2 * feat)
    arrived = lax.all_to_all(packed, "wide", split_axis=0, concat_axis=0, tiled=True)
    arrived = arrived.reshape(wide_count * slot_count, hid + 2 * feat)
    return (
        query_grad,
        arrived[:, hid : hid + feat],
        arrived[:, :hid],
        arrived[:, hid + feat :],
    )


def solution(mesh):
    return jax.shard_map(
        shards,
        mesh=mesh,
        in_specs=(
            P(("wide", "blk"), None),
            P(("wide", "blk"), None),
            P("wide"),
            P("wide"),
            P("wide", None),
            P("wide", None),
            P("wide", "blk"),
            P("wide", "blk"),
            P("blk", None),
            P("blk"),
        ),
        out_specs=(P(("wide", "blk"), None), P("wide", "blk"), P("wide", "blk"), P("wide", "blk")),
        check_vma=False,
    )
```

time: 410 us -> 142 us (0.35)
  the two profiles are of different devices: /device:TPU:62 before, /device:TPU:9 now
where the time goes in v1:
time: 142 us; the launch traced here: 141 us
  Pallas kernels  57.9 us (41%)
  waiting for transfers between devices  43.4 us (31%)
  starting transfers between devices  27.9 us (20%)
  local copies, waits for them, and re-layouts  9.58 us (7%)
    pallas_call x1, Pallas kernels, layer(): pl.pallas_call(kernel, out_shape=(jax.ShapeDtypeStruct(query_emb.shape, B...  57.9 us
    all_to_all x1, waiting for transfers between devices, shards(): lax.all_to_all(packed, 'wide', split_axis=0, concat_axis=0, tiled=True)  43.4 us
    all_to_all x1, starting transfers between devices, shards(): lax.all_to_all(packed, 'wide', split_axis=0, concat_axis=0, tiled=True)  27.9 us
    unnamed x17, local copies, waits for them, and re-layouts  6.62 us
  transfers between devices with their start and end apart: 1, of which 1 were waited for; matrix products, arithmetic and copies ran while one was open for 0% of the time, Pallas kernels for 0%

profile of v1, /device:TPU:9, one launch (start us, length us, event | category | flops | bytes accessed | tf_op | source)
XLA Modules:
  0.0 141.4 jit_solution(7624006432324766041)
XLA Ops:
  0.6 0.9 fusion
  1.6 0.7 multiply_add_fusion
  2.3 0.0 copy-start
  2.3 1.0 copy-done
  3.2 0.0 copy-start.1
  3.2 0.9 copy-done.1
  4.1 0.0 copy-start.2
  4.1 0.8 copy-done.2
  4.9 0.0 copy-start.3
  4.9 0.8 copy-done.3
  5.6 0.0 copy-start.4
  5.6 0.7 copy-done.4
  6.3 0.0 copy-start.5
  6.3 0.7 copy-done.5
  7.0 0.0 copy-start.6
  7.0 0.7 copy-done.6
  7.6 0.0 copy-start.7
  7.6 0.7 copy-done.7
  8.3 57.9 %shard_map.129 = (bf16[4,4096]{1,0:T(4,128)(2,1)S(1)}, bf16[192,1280]{1,0:T(8,128)(2,1)S(1)}) custom-call(bf16[4,4096]{1,0:T(4,128)(2,1)S(1)} %copy-done.2, bf16[4,4096]{1,0:T(4,128)(2,1)S(1)} %copy-done.3, f32[1,64]{1,0:T(1,128)S(1)} %bitcast.6, s32[1,64]{1,0:T(1,128)S(1)} %bitcast.7, s32[1,64]{1,0:T(1,128)S(1)} %copy-done.7, f32[1,256]{1,0:T(1,128)S(1)} %bitcast.5, ...), custom_call_target="tpu_custom_call" | custom-call | tf_op jit(solution)/shard_map/pallas_call | solution.py:380
  66.2 0.4 convolution_convert_fusion
  66.5 1.2 reshape.23
  67.7 27.9 %all-to-all-start = ((bf16[48,6,1280]{2,1,0:T(8,128)(2,1)}), bf16[48,6,1280]{2,1,0:T(8,128)(2,1)S(1)}, u32[]{:S(2)}, u32[]{:S(2)}) async-start(bf16[48,6,1280]{2,1,0:T(8,128)(2,1)} %reshape.23), calls=%async_computation | async-start | bytes 1966080 | tf_op jit(solution)/shard_map/all_to_all | solution.py:447
  95.6 43.4 %all-to-all-done = bf16[48,6,1280]{2,1,0:T(8,128)(2,1)S(1)} async-done(((bf16[48,6,1280]{2,1,0:T(8,128)(2,1)}), bf16[48,6,1280]{2,1,0:T(8,128)(2,1)S(1)}, u32[]{:S(2)}, u32[]{:S(2)}) %all-to-all-start) | async-done | bytes 737312 | tf_op jit(solution)/shard_map/all_to_all | solution.py:447
  139.0 0.2 reshape.24
  139.3 0.7 fusion.3
  140.0 0.8 slice.13
  140.8 0.6 copy.15
Async XLA Ops:
  2.3 1.0 copy-start
  3.2 0.9 copy-start.1
  4.1 0.8 copy-start.2
  4.9 0.8 copy-start.3
  5.6 0.7 copy-start.4
  6.3 0.7 copy-start.5
  7.0 0.7 copy-start.6
  7.6 0.7 copy-start.7
  67.7 71.3 %all-to-all-start = ((bf16[48,6,1280]{2,1,0:T(8,128)(2,1)}), bf16[48,6,1280]{2,1,0:T(8,128)(2,1)S(1)}, u32[]{:S(2)}, u32[]{:S(2)}) async-start(bf16[48,6,1280]{2,1,0:T(8,128)(2,1)} %reshape.23), calls=%async_computation | async-start | bytes 1966080 | tf_op jit(solution)/shard_map/all_to_all | solution.py:447
